TPU v7x, 512 devices: a whole 4x8x8 slice. The times are simulated.
512 devices in a mesh: prow: 16 (over y, core), pcol: 32 (over z, x).
Axes of the slice: x: 4, y: 8, z: 8, core: 2. Of those that a mesh axis runs over, the one named last changes fastest.
Arguments:
- stiffness: float32 [4, 16, 2, 32, 256, 256], P(None, 'prow', None, 'pcol'), may hold values from -1 to 33, as said below
- pattern: int32 [2, 64], replicated, may hold values 0 or 1
Outputs:
- factored: float32 [4, 16, 2, 32, 256, 256], P(None, 'prow', None, 'pcol')
Inputs may be any that keep to these rules, and one draw needn't show every extreme that they name: `stiffness`: Symmetric; entries off the main diagonal have magnitude at most 1, and the main diagonal's entries lie between 31 and 33.
All inputs are finite; a program needn't handle non-finite values.
Results may differ from a plain program's by a relative error of at most 0.0003.
Values sent between devices are 32-bit elements; how exact they have to be, the bound alone decides.
A program may use at most 64 MiB of HBM per device.

v0:
```python
import jax
import jax.numpy as jnp
from jax import lax
from jax.sharding import PartitionSpec as P


def broadcast(block, axis, source):
    block = jnp.where(lax.axis_index(axis) == source, block, jnp.zeros_like(block))
    return lax.psum(block, axis)


def solve_blocks(factor, blocks):
    count = blocks.shape[0]
    order = blocks.shape[1]
    right_hand = jnp.transpose(blocks, (2, 0, 1)).reshape(order, count * order)
    solved = lax.linalg.triangular_solve(factor, right_hand, left_side=True, lower=True)
    return jnp.transpose(solved.reshape(order, count, order), (1, 2, 0))


def local(stiffness, pattern):
    row_count = stiffness.shape[0]
    col_count = stiffness.shape[2]
    order = stiffness.shape[4]
    nprow = lax.axis_size("prow")
    npcol = lax.axis_size("pcol")
    my_row = lax.axis_index("prow")
    my_col = lax.axis_index("pcol")
    blocks = stiffness.reshape(row_count, col_count, order, order)
    glob_rows = my_row + nprow * jnp.arange(row_count, dtype=jnp.int32)
    glob_cols = my_col + npcol * jnp.arange(col_count, dtype=jnp.int32)
    all_rows = jnp.arange(row_count * nprow, dtype=jnp.int32)
    first_flags = (pattern[0] == 1) & (all_rows > 0)
    second_flags = ((pattern[1] == 1) | first_flags[1] & first_flags) & (all_rows > 1)
    for column, flags in ((0, first_flags), (1, second_flags)):
        local_col = column // npcol
        local_diag = blocks[column // nprow, local_col]
        factor = broadcast(jnp.linalg.cholesky(local_diag), "prow", column % nprow)
        payload = solve_blocks(factor, blocks[:, local_col])
        row_pieces = broadcast(payload, "pcol", column % npcol)
        my_flags = jnp.take(flags, glob_rows)
        panel_blocks = jnp.where(my_flags[:, None, None], row_pieces, jnp.zeros_like(row_pieces))
        source_rows = glob_cols // nprow
        column_pieces = broadcast(
            jnp.take(panel_blocks, source_rows, axis=0), "prow", my_col % nprow
        )
        update = jnp.einsum(
            "iab,jcb->ijac", panel_blocks, column_pieces, precision=lax.Precision.HIGHEST
        )
        keep_mask = (glob_cols[None, :] > column) & (glob_cols[None, :] <= glob_rows[:, None])
        blocks = blocks - jnp.where(keep_mask[:, :, None, None], update, jnp.zeros_like(update))
        old_column = blocks[:, local_col]
        new_column = jnp.where((glob_rows > column)[:, None, None], panel_blocks, old_column)
        new_column = jnp.where((glob_rows == column)[:, None, None], factor[None, :, :], new_column)
        is_panel_col = my_col == column % npcol
        blocks = blocks.at[:, local_col].set(jnp.where(is_panel_col, new_column, old_column))
    return blocks.reshape(stiffness.shape)


def solution(mesh):
    placed = (P(None, "prow", None, "pcol", None, None), P())
    return jax.shard_map(
        local,
        mesh=mesh,
        in_specs=placed,
        out_specs=P(None, "prow", None, "pcol", None, None),
        check_vma=False,
    )
```

profile of v0, /device:TPU:1, one launch (start us, length us, event | category | flops | bytes accessed | tf_op | source)
XLA Modules:
  0.0 959.3 jit_solution(15155828020917416587)
XLA Ops:
  6.5 1.9 copy.15
  8.7 11.7 %cholesky.130 = f32[128,128]{1,0:T(8,128)S(1)} custom-call(f32[128,128]{1,0:T(8,128)S(1)} %cholesky.194), custom_call_target="Cholesky" | custom-call | tf_op jit(solution)/shard_map/jit(cholesky)/cholesky | solution.py:37
  20.5 9.8 %custom-call.13 = f32[1,128,128]{1,2,0:T(8,128)S(1)} custom-call(f32[1,128,128]{2,1,0:T(8,128)S(1)} %get-tuple-element.76), custom_call_target="InvertDiagBlocksLowerTriangular" | custom-call | tf_op jit(solution)/shard_map/jit(cholesky)/cholesky | solution.py:37
  30.8 11.7 %cholesky.147 = f32[128,128]{1,0:T(8,128)S(1)} custom-call(f32[128,128]{1,0:T(8,128)S(1)} %convolution_subtract_fusion.3), custom_call_target="Cholesky" | custom-call | tf_op jit(solution)/shard_map/jit(cholesky)/cholesky | solution.py:37
  42.5 0.7 compare_reduce_fusion.2
  44.6 0.7 fusion.15
  45.3 12.5 %all-reduce.10.cloned.1.call-start = ((), (), s32[]{:S(2)}) async-start(), calls=%async_computation.1 | async-start | bytes 2097152 | tf_op jit(solution)/shard_map/psum | solution.py:9
  57.9 1.0 slice_bitcast_fusion.2
  58.9 1.6 copy.17
  60.5 104.2 %all-reduce.8.cloned.1.call-done = f32[256,256]{1,0:T(8,128)} async-done(((f32[256,256]{1,0:T(8,128)}), f32[256,256]{1,0:T(8,128)}) %all-reduce.8.cloned.1.call-update) | async-done | bytes 262160 | tf_op jit(solution)/shard_map/psum | solution.py:9
  164.8 1.0 fusion.14
  165.8 4.1 while.6
  166.4 1.4 bitcast_dynamic-update-slice_fusion.6
  168.5 1.4 bitcast_dynamic-update-slice_fusion.6
  170.6 20.5 %custom-call.14 = f32[2,128,128]{1,2,0:T(8,128)S(1)} custom-call(f32[2,128,128]{2,1,0:T(8,128)} %copy-done.5), custom_call_target="InvertDiagBlocksLowerTriangular" | custom-call | tf_op jit(solution)/shard_map/triangular_solve/custom-call.0 | solution.py:16
  191.7 1.0 convolution_subtract_fusion.1
  193.5 1.3 copy.18
  194.8 2.6 copy.19
  198.3 156.5 %all-reduce.10.cloned.1.call-done = f32[4,256,256]{1,2,0:T(8,128)} async-done(((f32[4,256,256]{1,2,0:T(8,128)}), f32[4,256,256]{1,2,0:T(8,128)}) %all-reduce.10.cloned.1.call-update) | async-done | bytes 1048592 | tf_op jit(solution)/shard_map/psum | solution.py:9
  354.8 1.4 broadcast_select_fusion.1
  356.2 1.4 gather_fusion.1
  357.6 1.9 select_select_fusion.2
  359.7 1.1 copy.23
  360.8 115.4 %all-reduce.12.cloned.1.call-done = f32[2,256,256]{1,2,0:T(8,128)} async-done(((f32[2,256,256]{1,2,0:T(8,128)}), f32[2,256,256]{1,2,0:T(8,128)}) %all-reduce.12.cloned.1.call-update) | async-done | bytes 524304 | tf_op jit(solution)/shard_map/psum | solution.py:9
  476.2 3.2 fusion.1
  479.4 1.3 copy-done
  481.2 11.7 %cholesky.164 = f32[128,128]{1,0:T(8,128)S(1)} custom-call(f32[128,128]{1,0:T(8,128)S(1)} %cholesky.197), custom_call_target="Cholesky" | custom-call | tf_op jit(solution)/shard_map/jit(cholesky)/cholesky | solution.py:37
  492.9 0.7 compare_reduce_fusion.1
  493.6 9.8 %custom-call.15 = f32[1,128,128]{1,2,0:T(8,128)S(1)} custom-call(f32[1,128,128]{2,1,0:T(8,128)S(1)} %get-tuple-element.72), custom_call_target="InvertDiagBlocksLowerTriangular" | custom-call | tf_op jit(solution)/shard_map/jit(cholesky)/cholesky | solution.py:37
  504.0 11.9 %cholesky.181 = f32[128,128]{1,0:T(8,128)S(1)} custom-call(f32[128,128]{1,0:T(8,128)S(1)} %convolution_subtract_fusion.2), custom_call_target="Cholesky" | custom-call | tf_op jit(solution)/shard_map/jit(cholesky)/cholesky | solution.py:37
  517.8 0.7 select_select_fusion.3
  518.9 114.4 %all-reduce.14.cloned.1.call-done = f32[256,256]{1,0:T(8,128)} async-done(((f32[256,256]{1,0:T(8,128)}), f32[256,256]{1,0:T(8,128)}) %all-reduce.14.cloned.1.call-update) | async-done | bytes 262160 | tf_op jit(solution)/shard_map/psum | solution.py:9
  633.3 1.0 fusion.12
  634.3 4.1 while.7
  634.9 1.4 bitcast_dynamic-update-slice_fusion.7
  636.9 1.4 bitcast_dynamic-update-slice_fusion.7
  638.4 19.7 %custom-call.16 = f32[2,128,128]{1,2,0:T(8,128)S(1)} custom-call(f32[2,128,128]{2,1,0:T(8,128)S(1)} %get-tuple-element.48), custom_call_target="InvertDiagBlocksLowerTriangular" | custom-call | tf_op jit(solution)/shard_map/triangular_solve/custom-call.0 | solution.py:16
  658.7 1.0 convolution_subtract_fusion
  660.5 1.3 copy.26
  661.8 2.6 copy.27
  666.4 155.4 %all-reduce.16.cloned.1.call-done = f32[4,256,256]{1,2,0:T(8,128)} async-done(((f32[4,256,256]{1,2,0:T(8,128)}), f32[4,256,256]{1,2,0:T(8,128)}) %all-reduce.16.cloned.1.call-update) | async-done | bytes 1048592 | tf_op jit(solution)/shard_map/psum | solution.py:9
  821.8 2.4 broadcast_select_fusion
  824.2 2.6 gather_fusion.3
  826.8 2.0 select_select_fusion.1
  829.1 116.4 %all-reduce.18.cloned.1.call-done = f32[2,256,256]{1,2,0:T(8,128)} async-done(((f32[2,256,256]{1,2,0:T(8,128)}), f32[2,256,256]{1,2,0:T(8,128)}) %all-reduce.18.cloned.1.call-update) | async-done | bytes 524304 | tf_op jit(solution)/shard_map/psum | solution.py:9
  945.5 3.4 fusion
  949.0 1.1 copy-done.3
  950.3 1.8 copy.32
  (84 shorter events, 12.2 us)
Async XLA Ops:
  6.5 158.2 %all-reduce.8.cloned.1.call-start = ((), (), s32[]{:S(2)}) async-start(), calls=%async_computation | async-start | bytes 524288 | tf_op jit(solution)/shard_map/psum | solution.py:9
  8.7 50.3 %copy-start.6 = (s32[2,64]{1,0:T(2,128)S(1)}, s32[2,64]{1,0:T(2,128)}, u32[]{:S(2)}) copy-start(s32[2,64]{1,0:T(2,128)} %param.14) | copy-start | bytes 1540
  45.3 309.5 %all-reduce.10.cloned.1.call-start = ((), (), s32[]{:S(2)}) async-start(), calls=%async_computation.1 | async-start | bytes 2097152 | tf_op jit(solution)/shard_map/psum | solution.py:9
  169.9 0.7 copy-start.5
  197.4 278.8 %all-reduce.12.cloned.1.call-start = ((), (), s32[]{:S(2)}) async-start(), calls=%async_computation.2 | async-start | bytes 1048576 | tf_op jit(solution)/shard_map/psum | solution.py:9
  359.5 273.8 %all-reduce.14.cloned.1.call-start = ((), (), s32[]{:S(2)}) async-start(), calls=%async_computation.3 | async-start | bytes 524288 | tf_op jit(solution)/shard_map/psum | solution.py:9
  476.2 4.5 copy-start.2
  479.4 1.3 copy-start
  518.5 303.2 %all-reduce.16.cloned.1.call-start = ((), (), s32[]{:S(2)}) async-start(), calls=%async_computation.4 | async-start | bytes 2097152 | tf_op jit(solution)/shard_map/psum | solution.py:9
  664.4 281.1 %all-reduce.18.cloned.1.call-start = ((), (), s32[]{:S(2)}) async-start(), calls=%async_computation.5 | async-start | bytes 1048576 | tf_op jit(solution)/shard_map/psum | solution.py:9
  666.3 162.5 %copy-start.1 = (f32[4,2,256,256]{2,3,0,1:T(8,128)S(1)}, f32[4,2,256,256]{2,3,0,1:T(8,128)}, u32[]{:S(2)}) copy-start(f32[4,2,256,256]{2,3,0,1:T(8,128)} %copy-done) | copy-start | bytes 6291460
  826.8 2.1 copy-start.4
  948.9 1.2 copy-start.3
Sparse Core Ops, SparseCore 0:
  45.5 119.2 all-reduce.7
  197.6 157.2 all-reduce.9
  359.7 116.4 all-reduce.11
  518.6 114.6 all-reduce.13
  664.5 157.1 all-reduce.15
  828.9 116.4 all-reduce.17
where the time goes:
time: 968 us; the launch traced here: 959 us
  waiting for transfers between devices  763 us (79%)
  other arithmetic  122 us (13%)
  local copies, waits for them, and re-layouts  33.3 us (3%)
  between operations  16.9 us (2%)
  starting transfers between devices  12.7 us (1%)
  matrix products  12 us (1%)
    psum x6, waiting for transfers between devices, broadcast(): return lax.psum(block, axis)  762 us
    another operation x13, other arithmetic, local(): factor = broadcast(jnp.linalg.cholesky(local_diag), 'prow', column % nprow)  68.9 us
    another operation x5, other arithmetic, solve_blocks(): lax.linalg.triangular_solve(factor, right_hand, left_side=True, lower=True)  42.1 us
  transfers between devices with their start and end apart: 6, of which 6 were waited for; matrix products, arithmetic and copies ran while one was open for 1% of the time, Pallas kernels for 0%

commit v1 on v0

--- a/solution.py
+++ b/solution.py
@@ -6,7 +6,10 @@
 
 def broadcast(block, axis, source):
     block = jnp.where(lax.axis_index(axis) == source, block, jnp.zeros_like(block))
-    return lax.psum(block, axis)
+    report_vector_over_axis = lambda q_in, mesh_dim: jnp.sum(
+        lax.all_gather(q_in, axis_name=mesh_dim), axis=0
+    )
+    return report_vector_over_axis(block, axis)
 
 
 def solve_blocks(factor, blocks):

time: 968 us -> 913 us (0.943)
  waiting for transfers between devices: 763 us -> 671 us
  other arithmetic: 122 us -> 161 us
  starting transfers between devices: 12.7 us -> 0.85 us
    psum x6 -> x0, waiting for transfers between devices: 762 us -> none  [broadcast(): return lax.psum(block, axis)]
    all_gather x0 -> x6, waiting for transfers between devices: none -> 671 us  [broadcast(): lax.all_gather(q_in, axis_name=mesh_dim)]
    reduce_sum x0 -> x6, other arithmetic: none -> 39.5 us  [broadcast(): jnp.sum(lax.all_gather(q_in, axis_name=mesh_dim), axis=0)]
    psum x6 -> x0, starting transfers between devices: 12.7 us -> none  [broadcast(): return lax.psum(block, axis)]
where the time goes in v1:
time: 913 us; the launch traced here: 905 us
  waiting for transfers between devices  671 us (73%)
  other arithmetic  161 us (18%)
  local copies, waits for them, and re-layouts  40.8 us (4%)
  between operations  16.7 us (2%)
  matrix products  14.8 us (2%)
    all_gather x6, waiting for transfers between devices, broadcast(): lax.all_gather(q_in, axis_name=mesh_dim)  671 us
    another operation x13, other arithmetic, local(): factor = broadcast(jnp.linalg.cholesky(local_diag), 'prow', column % nprow)  69.9 us
    another operation x5, other arithmetic, solve_blocks(): lax.linalg.triangular_solve(factor, right_hand, left_side=True, lower=True)  40.9 us
    reduce_sum x6, other arithmetic, broadcast(): jnp.sum(lax.all_gather(q_in, axis_name=mesh_dim), axis=0)  39.5 us
  transfers between devices with their start and end apart: 6, of which 6 were waited for; matrix products, arithmetic and copies ran while one was open for 1% of the time, Pallas kernels for 0%

profile of v1, /device:TPU:1, one launch (start us, length us, event | category | flops | bytes accessed | tf_op | source)
XLA Modules:
  0.0 904.5 jit_solution(850210557994261556)
XLA Ops:
  6.5 1.9 copy.35
  8.7 11.7 %cholesky.130 = f32[128,128]{1,0:T(8,128)S(1)} custom-call(f32[128,128]{1,0:T(8,128)S(1)} %cholesky.194), custom_call_target="Cholesky" | custom-call | tf_op jit(solution)/shard_map/jit(cholesky)/cholesky | solution.py:40
  20.5 9.8 %custom-call.13 = f32[1,128,128]{1,2,0:T(8,128)S(1)} custom-call(f32[1,128,128]{2,1,0:T(8,128)S(1)} %get-tuple-element.78), custom_call_target="InvertDiagBlocksLowerTriangular" | custom-call | tf_op jit(solution)/shard_map/jit(cholesky)/cholesky | solution.py:40
  30.8 11.7 %cholesky.147 = f32[128,128]{1,0:T(8,128)S(1)} custom-call(f32[128,128]{1,0:T(8,128)S(1)} %convolution_subtract_fusion.3), custom_call_target="Cholesky" | custom-call | tf_op jit(solution)/shard_map/jit(cholesky)/cholesky | solution.py:40
  45.8 1.0 slice_bitcast_fusion.1
  46.8 1.6 copy.37
  48.6 47.2 %all-gather.13.cloned.1.call-done = f32[4096,256]{1,0:T(8,128)} async-done(((f32[256,256]{1,0:T(8,128)}), f32[4096,256]{1,0:T(8,128)}) %all-gather.13.cloned.1.call-update) | async-done | bytes 4194320 | tf_op jit(solution)/shard_map/all_gather | solution.py:10
  95.9 2.5 reduce_sum.58
  98.5 3.9 while.6
  99.1 1.3 bitcast_dynamic-update-slice_fusion.5
  101.1 1.3 bitcast_dynamic-update-slice_fusion.5
  102.9 19.7 %custom-call.14 = f32[2,128,128]{1,2,0:T(8,128)S(1)} custom-call(f32[2,128,128]{2,1,0:T(8,128)S(1)} %get-tuple-element.47), custom_call_target="InvertDiagBlocksLowerTriangular" | custom-call | tf_op jit(solution)/shard_map/triangular_solve/custom-call.0 | solution.py:19
  124.6 1.3 copy.71
  126.8 237.3 %all-gather.15.cloned.1.call-done = f32[128,256,256]{2,1,0:T(8,128)} async-done(((f32[4,256,256]{2,1,0:T(8,128)}), f32[128,256,256]{2,1,0:T(8,128)}) %all-gather.15.cloned.1.call-update) | async-done | bytes 33554448 | tf_op jit(solution)/shard_map/all_gather | solution.py:10
  364.1 12.0 %reduce_sum.59 = f32[4,256,256]{2,1,0:T(8,128)S(1)} reduce(f32[32,4,256,256]{3,2,1,0:T(8,128)} %bitcast.160, f32[]{:T(128)} %constant.175.clone.1), dimensions={0}, to_apply=%region_5.9 | reduce | flops 8126464 | bytes 34603012 | tf_op jit(solution)/shard_map/reduce_sum | solution.py:9
  376.6 1.4 gather_fusion.1
  377.9 1.2 select_select_fusion.1
  381.1 54.8 %all-gather.17.cloned.1.call-done = f32[32,256,256]{2,1,0:T(8,128)} async-done(((f32[2,256,256]{2,1,0:T(8,128)}), f32[32,256,256]{2,1,0:T(8,128)}) %all-gather.17.cloned.1.call-update) | async-done | bytes 8388624 | tf_op jit(solution)/shard_map/all_gather | solution.py:10
  435.8 4.8 reduce_sum.60
  440.6 4.0 fusion.1
  444.6 1.2 fusion.8
  447.9 1.1 copy.49
  450.7 11.7 %cholesky.164 = f32[128,128]{1,0:T(8,128)S(1)} custom-call(f32[128,128]{1,0:T(8,128)S(1)} %cholesky.197), custom_call_target="Cholesky" | custom-call | tf_op jit(solution)/shard_map/jit(cholesky)/cholesky | solution.py:40
  462.9 9.8 %custom-call.15 = f32[1,128,128]{1,2,0:T(8,128)S(1)} custom-call(f32[1,128,128]{2,1,0:T(8,128)S(1)} %get-tuple-element.74), custom_call_target="InvertDiagBlocksLowerTriangular" | custom-call | tf_op jit(solution)/shard_map/jit(cholesky)/cholesky | solution.py:40
  473.8 1.1 convolution_subtract_fusion.2
  474.9 11.9 %cholesky.181 = f32[128,128]{1,0:T(8,128)S(1)} custom-call(f32[128,128]{1,0:T(8,128)S(1)} %convolution_subtract_fusion.2), custom_call_target="Cholesky" | custom-call | tf_op jit(solution)/shard_map/jit(cholesky)/cholesky | solution.py:40
  486.8 1.2 compare_reduce_fusion.1
  490.7 1.3 copy.51
  492.0 1.1 slice.170
  494.1 40.3 %all-gather.19.cloned.1.call-done = f32[4096,256]{1,0:T(8,128)} async-done(((f32[256,256]{1,0:T(8,128)}), f32[4096,256]{1,0:T(8,128)}) %all-gather.19.cloned.1.call-update) | async-done | bytes 4194320 | tf_op jit(solution)/shard_map/all_gather | solution.py:10
  534.4 2.6 reduce_sum.62
  537.7 6.7 while.7
  539.0 2.2 bitcast_dynamic-update-slice_fusion.6
  542.4 2.1 bitcast_dynamic-update-slice_fusion.6
  545.1 20.5 %custom-call.16 = f32[2,128,128]{1,2,0:T(8,128)S(1)} custom-call(f32[2,128,128]{2,1,0:T(8,128)} %copy-done.7), custom_call_target="InvertDiagBlocksLowerTriangular" | custom-call | tf_op jit(solution)/shard_map/triangular_solve/custom-call.0 | solution.py:19
  566.3 1.7 convolution_subtract_fusion
  568.7 1.3 copy.75
  572.0 236.2 %all-gather.21.cloned.1.call-done = f32[128,256,256]{2,1,0:T(8,128)} async-done(((f32[4,256,256]{2,1,0:T(8,128)}), f32[128,256,256]{2,1,0:T(8,128)}) %all-gather.21.cloned.1.call-update) | async-done | bytes 33554448 | tf_op jit(solution)/shard_map/all_gather | solution.py:10
  808.2 12.9 %reduce_sum.63 = f32[4,256,256]{2,1,0:T(8,128)} reduce(f32[32,4,256,256]{3,2,1,0:T(8,128)} %bitcast.161, f32[]{:T(128)} %constant.175.clone.1), dimensions={0}, to_apply=%region_8.13 | reduce | flops 8126464 | bytes 34603012 | tf_op jit(solution)/shard_map/reduce_sum | solution.py:9
  821.1 1.6 copy.55
  822.7 1.1 broadcast_select_fusion
  823.8 2.6 gather_fusion.3
  826.4 1.9 select_select_fusion
  828.3 2.1 copy.56
  831.3 54.9 %all-gather.23.cloned.1.call-done = f32[32,256,256]{2,1,0:T(8,128)} async-done(((f32[2,256,256]{2,1,0:T(8,128)}), f32[32,256,256]{2,1,0:T(8,128)}) %all-gather.23.cloned.1.call-update) | async-done | bytes 8388624 | tf_op jit(solution)/shard_map/all_gather | solution.py:10
  886.2 4.8 reduce_sum.64
  891.0 3.4 fusion
  895.6 1.8 copy.64
  (105 shorter events, 27.0 us)
Async XLA Ops:
  6.5 89.3 %all-gather.13.cloned.1.call-start = ((), (), s32[]{:S(2)}) async-start(), calls=%async_computation | async-start | bytes 4456448 | tf_op jit(solution)/shard_map/all_gather | solution.py:10
  8.5 38.4 %copy-start = (f32[4,1,2,1,256,256]{4,5,2,0,3,1:T(8,128)}, f32[4,1,2,1,256,256]{4,5,2,0,3,1:T(8,128)S(1)}, u32[]{:S(2)}) copy-start(f32[4,1,2,1,256,256]{4,5,2,0,3,1:T(8,128)S(1)} %copy.35) | copy-start | bytes 6291460
  45.3 318.8 %all-gather.15.cloned.1.call-start = ((), (), s32[]{:S(2)}) async-start(), calls=%async_computation.1 | async-start | bytes 34603008 | tf_op jit(solution)/shard_map/all_gather | solution.py:10
  102.4 0.5 copy-start.11
  124.6 1.4 copy-start.9
  125.9 309.9 %all-gather.17.cloned.1.call-start = ((), (), s32[]{:S(2)}) async-start(), calls=%async_computation.2 | async-start | bytes 8912896 | tf_op jit(solution)/shard_map/all_gather | solution.py:10
  376.6 4.5 copy-start.1
  380.1 154.3 %all-gather.19.cloned.1.call-start = ((), (), s32[]{:S(2)}) async-start(), calls=%async_computation.3 | async-start | bytes 4456448 | tf_op jit(solution)/shard_map/all_gather | solution.py:10
  446.2 1.0 copy-start.4
  446.2 44.5 %copy-start.2 = (f32[256,4,256]{2,0,1:T(8,128)S(1)}, f32[256,4,256]{2,0,1:T(8,128)}, u32[]{:S(2)}) copy-start(f32[256,4,256]{2,0,1:T(8,128)} %fusion.8) | copy-start | bytes 3145732
  449.9 0.7 copy-start.6
  490.7 317.5 %all-gather.21.cloned.1.call-start = ((), (), s32[]{:S(2)}) async-start(), calls=%async_computation.4 | async-start | bytes 34603008 | tf_op jit(solution)/shard_map/all_gather | solution.py:10
  534.4 31.2 %copy-start.3 = (f32[256,4,256]{0,2,1:T(8,128)S(1)}, f32[256,4,256]{0,2,1:T(8,128)}, u32[]{:S(2)}) copy-start(f32[256,4,256]{0,2,1:T(8,128)} %copy.51) | copy-start | bytes 3145732
  544.5 0.6 copy-start.7
  568.7 2.0 copy-start.10
  570.0 316.1 %all-gather.23.cloned.1.call-start = ((), (), s32[]{:S(2)}) async-start(), calls=%async_computation.5 | async-start | bytes 8912896 | tf_op jit(solution)/shard_map/all_gather | solution.py:10
  886.2 4.8 copy-start.8
  894.4 1.0 copy-start.5
Sparse Core Ops, SparseCore 0:
  45.4 50.4 all-gather.12
  126.0 237.9 all-gather.14
  380.2 55.5 all-gather.16
  490.8 43.5 all-gather.18
  570.2 237.9 all-gather.20
  830.5 55.5 all-gather.22
